TPU v7x, 256 devices: a whole 4x4x8 slice. The times are simulated.
256 devices in a mesh: space: 32 (over x, z), col: 8 (over y, core).
Axes of the slice: x: 4, y: 4, z: 8, core: 2. Of those that a mesh axis runs over, the one named last changes fastest.
Arguments:
- blocks: bfloat16 [2560, 24, 128, 128], P('space', 'col'), may hold values from -0.109375 to 0.109375
- basis_tiles: bfloat16 [2560, 128, 128], P('space'), may hold values from -6 to 6
- weights: float32 [2560, 128], P('space'), may hold values from 0.1 to 1
- neighbour_device: int32 [2560, 24], P('space', 'col'), may hold values from 0 to 31, as said below
- neighbour_row: int32 [2560, 24], P('space', 'col'), may hold values from 0 to 79
- counts: int32 [2560], P('space'), may hold values from 12 to 24
- aggregate: int32 [2560], P('space'), may hold values from 0 to 9
- pair_slot: int32 [2560, 24], P('space', 'col'), may hold values from 0 to 3
Outputs:
- coarse: float32 [1280, 128, 128], P(('space', 'col'))
Inputs may be any that keep to these rules, and one draw needn't show every extreme that they name: `neighbour_device`: among the slots of one device's 80 rows that fall to one index of col, exactly 60 name another device; no other device is named more than 3 times there, and some other device exactly 3 times.
All inputs are finite; a program needn't handle non-finite values.
Results may differ from a plain program's by a relative error of at most 0.0045.
Values may be sent and summed in bfloat16 or wider, within the bound.
A program may use at most 128 MiB of HBM per device.

v0:
```python
import jax
import jax.numpy as jnp
from jax import lax
from jax.sharding import PartitionSpec as P

KC = 4
CAP = 3
NCD = 10


def per_device(
    blocks, basis_tiles, weights, neighbour_device, neighbour_row, counts, aggregate, pair_slot
):
    space_count = lax.axis_size("space")
    own_index = lax.axis_index("space")
    col_index = lax.axis_index("col")
    row_count, slot_count = neighbour_device.shape
    block_size = blocks.shape[2]
    coarse_size = basis_tiles.shape[2]
    slot_total = row_count * slot_count
    peer_of = neighbour_device.reshape(slot_total)
    row_of = neighbour_row.reshape(slot_total)
    remote = peer_of != own_index
    onehot = (
        (peer_of[:, None] == jnp.arange(space_count, dtype=jnp.int32)[None, :]) & remote[:, None]
    ).astype(jnp.int32)
    position = jnp.sum((jnp.cumsum(onehot, axis=0) - onehot) * onehot, axis=1)
    bucket = jnp.where(remote, peer_of * CAP + position, space_count * CAP)
    requests = jnp.zeros((space_count * CAP,), jnp.int32).at[bucket].set(row_of, mode="drop")
    requests = requests.reshape(space_count, CAP)
    asked_rows = lax.all_to_all(requests, "space", split_axis=0, concat_axis=0, tiled=True)
    tile_index = jnp.where(remote, row_count + bucket, row_of)
    received = lax.all_to_all(
        basis_tiles[asked_rows], "space", split_axis=0, concat_axis=0, tiled=True
    )
    tile_table = jnp.concatenate(
        [basis_tiles, received.reshape(space_count * CAP, block_size, coarse_size)], axis=0
    )
    fetched = tile_table[tile_index].reshape(row_count, slot_count, block_size, coarse_size)
    slot_number = col_index * slot_count + jnp.arange(slot_count, dtype=jnp.int32)
    usable = slot_number[None, :] < counts[:, None]
    masked = jnp.where(usable[:, :, None, None], blocks, jnp.zeros((), blocks.dtype))
    partial_sum = jnp.einsum("rkab,rkbc->rac", masked, fetched, preferred_element_type=jnp.float32)
    smoothed = lax.psum(partial_sum, "col")
    prolong = (basis_tiles.astype(jnp.float32) - weights[:, :, None] * smoothed).astype(
        jnp.bfloat16
    )
    received_prolong = lax.all_to_all(
        prolong[asked_rows], "space", split_axis=0, concat_axis=0, tiled=True
    )
    prolong_table = jnp.concatenate(
        [prolong, received_prolong.reshape(space_count * CAP, block_size, coarse_size)], axis=0
    )
    neighbour_prolong = prolong_table[tile_index].reshape(
        row_count, slot_count, block_size, coarse_size
    )
    applied = jnp.einsum(
        "rkab,rkbc->rkac", masked, neighbour_prolong, preferred_element_type=jnp.float32
    ).astype(jnp.bfloat16)
    contribution = jnp.einsum(
        "rad,rkae->rkde", prolong, applied, preferred_element_type=jnp.float32
    )
    targets = (aggregate[:, None] * KC + pair_slot).reshape(slot_total)
    coarse_local = jax.ops.segment_sum(
        contribution.reshape(slot_total, coarse_size, coarse_size), targets, num_segments=NCD * KC
    )
    return lax.psum_scatter(coarse_local, "col", scatter_dimension=0, tiled=True)


def solution(mesh):
    return jax.shard_map(
        per_device,
        mesh=mesh,
        in_specs=(
            P("space", "col", None, None),
            P("space", None, None),
            P("space", None),
            P("space", "col"),
            P("space", "col"),
            P("space"),
            P("space"),
            P("space", "col"),
        ),
        out_specs=P(("space", "col"), None, None),
        check_vma=False,
    )
```

profile of v0, /device:TPU:6, one launch (start us, length us, event | category | flops | bytes accessed | tf_op | source)
XLA Modules:
  0.0 429.7 jit_solution(17318623963266410459)
XLA Ops:
  6.5 0.8 copy.26
  7.3 0.7 broadcast_multiply_fusion
  8.0 0.8 copy.29
  8.8 0.2 reshape.182
  8.9 0.2 reshape.224
  9.1 0.2 eq.22
  9.2 0.7 broadcast_compare_fusion.1
  10.0 0.6 reduce-window.6
  10.6 0.2 slice_reduce_fusion
  10.8 0.1 bitcast_bitcast_fusion
  10.9 0.1 copy.24
  11.0 0.2 ne.29
  11.2 0.1 copy.25
  11.3 0.2 mul.47
  11.5 1.3 scatter_custom_fusion
  12.8 0.1 all_to_all.14
  12.9 19.3 %all_to_all.22 = s32[32,1,3]{2,1,0:T(1,128)S(1)} all-to-all(s32[32,1,3]{2,1,0:T(1,128)S(1)} %bitcast.44), channel_id=1, replica_groups=mesh['space'=32,'col'=8] {'space'}, dimensions={0} | all-to-all | bytes 768 | tf_op jit(solution)/shard_map/all_to_all | solution.py:31
  32.3 0.1 copy.31
  32.4 0.1 copy.32
  32.4 0.1 reshape.190
  32.6 0.0 copy-start.4
  32.6 0.0 copy-start.1
  32.6 4.6 %gather_fusion = bf16[96,128,128]{2,1,0:T(8,128)(2,1)} fusion(bf16[80,128,128]{2,1,0:T(8,128)(2,1)} %param.9, s32[1024]{0:T(1024)S(1)} %pad_clamp_fusion.1), kind=kCustom, calls=%fused_computation | custom fusion | bytes 6291840 | tf_op jit(solution)/shard_map/gather | solution.py:34
  37.2 6.6 %all-to-all-start.1 = ((bf16[32,3,128,128]{3,2,1,0:T(8,128)(2,1)}), bf16[32,3,128,128]{3,2,1,0:T(8,128)(2,1)}, u32[]{:S(2)}, u32[]{:S(2)}) async-start(bf16[32,3,128,128]{3,2,1,0:T(8,128)(2,1)} %bitcast.41), calls=%async_computation.1 | async-start | bytes 6291456 | tf_op jit(solution)/shard_map/all_to_all | solution.py:33
  43.9 0.0 all-reduce.3.cloned.1.call-start
  43.9 0.0 copy-done.4
  44.0 0.1 broadcast_compare_fusion
  44.0 71.3 %all-to-all-done.1 = bf16[32,3,128,128]{3,2,1,0:T(8,128)(2,1)} async-done(((bf16[32,3,128,128]{3,2,1,0:T(8,128)(2,1)}), bf16[32,3,128,128]{3,2,1,0:T(8,128)(2,1)}, u32[]{:S(2)}, u32[]{:S(2)}) %all-to-all-start.1) | async-done | bytes 3145760 | tf_op jit(solution)/shard_map/all_to_all | solution.py:33
  115.3 0.0 copy-done.1
  115.3 4.9 %pad_maximum_fusion = bf16[176,128,128]{2,1,0:T(8,128)(2,1)} fusion(bf16[96,128,128]{2,1,0:T(8,128)(2,1)} %bitcast.6, bf16[80,128,128]{2,1,0:T(8,128)(2,1)S(1)} %copy-done.1), kind=kLoop, calls=%fused_computation.11 | loop fusion | flops 2883584 | bytes 11534336 | tf_op jit(solution)/shard_map/concatenate | solution.py:36
  120.2 11.1 %gather_fusion.1 = bf16[240,128,128]{2,1,0:T(8,128)(2,1)} fusion(bf16[176,128,128]{2,1,0:T(8,128)(2,1)} %pad_maximum_fusion, s32[1024]{0:T(1024)S(1)} %pad_clamp_fusion), kind=kCustom, calls=%fused_computation.1 | custom fusion | bytes 15729600 | tf_op jit(solution)/shard_map/gather | solution.py:39
  131.4 0.0 copy-start.2
  131.4 10.1 %fusion.8 = f32[80,128,128]{2,1,0:T(8,128)} fusion(bf16[80,3,128,128]{3,2,1,0:T(8,128)(2,1)} %bitcast.43, bf16[80,3,128,128]{3,2,1,0:T(8,128)(2,1)} %param.8, pred[80,3]{1,0:T(8,128)(4,1)S(1)} %broadcast_compare_fusion), kind=kOutput, calls=%fused_computation.17 | convolution fusion | flops 1010565120 | bytes 20971760 | tf_op jit(solution)/shard_map/rkab,rkbc->rac/dot_general | solution.py:43
  141.4 0.0 all-reduce.3.cloned.1.call-update
  141.4 79.2 %all-reduce.3.cloned.1.call-done = f32[80,128,128]{2,1,0:T(8,128)} async-done(((f32[80,128,128]{2,1,0:T(8,128)}), f32[80,128,128]{2,1,0:T(8,128)}) %all-reduce.3.cloned.1.call-update) | async-done | bytes 5242896 | tf_op jit(solution)/shard_map/psum | solution.py:44
  220.7 0.0 copy-done.2
  220.7 4.6 %subtract_convert_fusion = bf16[80,128,128]{2,1,0:T(8,128)(2,1)S(1)} fusion(f32[80,128,128]{2,1,0:T(8,128)} %all-reduce.3.cloned.1.call-done, bf16[80,128,128]{2,1,0:T(8,128)(2,1)} %param.9, f32[80,128]{1,0:T(8,128)S(1)} %copy-done.2), kind=kLoop, calls=%fused_computation.13 | loop fusion | flops 5242880 | bytes 10526720 | tf_op jit(solution)/shard_map/convert_element_type | solution.py:45
  225.3 0.0 copy-start.5
  225.3 0.0 copy-start.3
  225.3 2.7 gather_fusion.2
  228.0 10.2 %all-to-all-start.2 = ((bf16[32,3,128,128]{3,2,1,0:T(8,128)(2,1)}), bf16[32,3,128,128]{3,2,1,0:T(8,128)(2,1)}, u32[]{:S(2)}, u32[]{:S(2)}) async-start(bf16[32,3,128,128]{3,2,1,0:T(8,128)(2,1)} %bitcast.42), calls=%async_computation.2 | async-start | bytes 6291456 | tf_op jit(solution)/shard_map/all_to_all | solution.py:48
  238.3 0.2 reduce-scatter.2.cloned.1.call-start
  238.5 0.0 copy-done.5
  238.5 0.0 copy-done.3
  238.5 0.1 copy.23
  238.6 0.2 reshape.230
  238.8 71.7 %all-to-all-done.2 = bf16[32,3,128,128]{3,2,1,0:T(8,128)(2,1)} async-done(((bf16[32,3,128,128]{3,2,1,0:T(8,128)(2,1)}), bf16[32,3,128,128]{3,2,1,0:T(8,128)(2,1)}, u32[]{:S(2)}, u32[]{:S(2)}) %all-to-all-start.2) | async-done | bytes 3145760 | tf_op jit(solution)/shard_map/all_to_all | solution.py:48
  310.5 4.9 %pad_maximum_fusion.1 = bf16[176,128,128]{2,1,0:T(8,128)(2,1)} fusion(bf16[96,128,128]{2,1,0:T(8,128)(2,1)} %bitcast.12, bf16[80,128,128]{2,1,0:T(8,128)(2,1)S(1)} %subtract_convert_fusion), kind=kLoop, calls=%fused_computation.12 | loop fusion | flops 2883584 | bytes 11534336 | tf_op jit(solution)/shard_map/concatenate | solution.py:51
  315.4 11.1 %gather_fusion.3 = bf16[240,128,128]{2,1,0:T(8,128)(2,1)} fusion(bf16[176,128,128]{2,1,0:T(8,128)(2,1)} %pad_maximum_fusion.1, s32[1024]{0:T(1024)S(1)} %pad_clamp_fusion), kind=kCustom, calls=%fused_computation.3 | custom fusion | bytes 15729600 | tf_op jit(solution)/shard_map/gather | solution.py:54
  326.5 11.1 %fusion = f32[80,3,128,128]{3,2,1,0:T(8,128)} fusion(bf16[80,3,128,128]{3,2,1,0:T(8,128)(2,1)} %bitcast.40, bf16[80,3,128,128]{3,2,1,0:T(8,128)(2,1)} %param.8, pred[80,3]{1,0:T(8,128)(4,1)S(1)} %broadcast_compare_fusion, bf16[80,128,128]{2,1,0:T(8,128)(2,1)S(1)} %subtract_convert_fusion), kind=kOutput, calls=%fused_computation.6 | convolution fusion | flops 2021130240 | bytes 34078960 | tf_op jit(solution)/shard_map/rad,rkae->rkde/dot_general | solution.py:60
  337.6 15.7 %copy.35 = f32[240,128,128]{2,1,0:T(8,128)} copy(f32[240,128,128]{1,2,0:T(8,128)} %bitcast.39) | data formatting | bytes 31457280 | tf_op jit(solution)/shard_map/reshape | solution.py:65
  353.3 0.3 broadcast_in_dim.20
  353.6 31.5 %scatter_fusion = f32[40,128,128]{2,1,0:T(8,128)S(1)} fusion(f32[40,128,128]{2,1,0:T(8,128)S(1)} %broadcast_in_dim.20, s32[240]{0:T(256)S(1)} %reshape.230, f32[240,128,128]{2,1,0:T(8,128)} %copy.35), kind=kCustom, calls=%fused_computation.5 | custom fusion | flops 3932160 | bytes 47186880 | tf_op jit(solution)/shard_map/scatter-add | solution.py:64
  385.1 0.0 copy-start
  385.1 1.5 copy-done
  386.6 0.0 reduce-scatter.2.cloned.1.call-update
  386.7 36.2 %reduce-scatter.2.cloned.1.call-done = f32[5,128,128]{2,1,0:T(8,128)} async-done(((f32[40,128,128]{2,1,0:T(8,128)}), f32[5,128,128]{2,1,0:T(8,128)}) %reduce-scatter.2.cloned.1.call-update) | async-done | bytes 327696 | tf_op jit(solution)/shard_map/reduce_scatter | solution.py:67
  (13 shorter events, 0.2 us)
Async XLA Ops:
  32.6 11.4 %copy-start.4 = (s32[80]{0:T(128)S(1)}, s32[80]{0:T(128)}, u32[]{:S(2)}) copy-start(s32[80]{0:T(128)} %param.13) | copy-start | bytes 964
  32.6 82.7 %copy-start.1 = (bf16[80,128,128]{2,1,0:T(8,128)(2,1)S(1)}, bf16[80,128,128]{2,1,0:T(8,128)(2,1)}, u32[]{:S(2)}) copy-start(bf16[80,128,128]{2,1,0:T(8,128)(2,1)} %param.9) | copy-start | bytes 7864324
  37.2 78.1 %all-to-all-start.1 = ((bf16[32,3,128,128]{3,2,1,0:T(8,128)(2,1)}), bf16[32,3,128,128]{3,2,1,0:T(8,128)(2,1)}, u32[]{:S(2)}, u32[]{:S(2)}) async-start(bf16[32,3,128,128]{3,2,1,0:T(8,128)(2,1)} %bitcast.41), calls=%async_computation.1 | async-start | bytes 6291456 | tf_op jit(solution)/shard_map/all_to_all | solution.py:33
  43.9 176.8 %all-reduce.3.cloned.1.call-start = ((), (), s32[]{:S(2)}) async-start(), calls=%async_computation.4 | async-start | bytes 10485760 | tf_op jit(solution)/shard_map/psum | solution.py:44
  131.4 89.3 %copy-start.2 = (f32[80,128]{1,0:T(8,128)S(1)}, f32[80,128]{1,0:T(8,128)}, u32[]{:S(2)}) copy-start(f32[80,128]{1,0:T(8,128)} %param.10) | copy-start | bytes 122884
  225.3 13.2 %copy-start.5 = (s32[80]{0:T(128)S(1)}, s32[80]{0:T(128)}, u32[]{:S(2)}) copy-start(s32[80]{0:T(128)} %param.14) | copy-start | bytes 964
  225.3 13.2 %copy-start.3 = (s32[80,3]{0,1:T(4,128)S(1)}, s32[80,3]{0,1:T(4,128)}, u32[]{:S(2)}) copy-start(s32[80,3]{0,1:T(4,128)} %param.15) | copy-start | bytes 2884
  228.0 82.5 %all-to-all-start.2 = ((bf16[32,3,128,128]{3,2,1,0:T(8,128)(2,1)}), bf16[32,3,128,128]{3,2,1,0:T(8,128)(2,1)}, u32[]{:S(2)}, u32[]{:S(2)}) async-start(bf16[32,3,128,128]{3,2,1,0:T(8,128)(2,1)} %bitcast.42), calls=%async_computation.2 | async-start | bytes 6291456 | tf_op jit(solution)/shard_map/all_to_all | solution.py:48
  238.3 184.5 %reduce-scatter.2.cloned.1.call-start = ((), (), s32[]{:S(2)}) async-start(), calls=%async_computation.5 | async-start | bytes 2949120 | tf_op jit(solution)/shard_map/reduce_scatter | solution.py:67
  385.1 1.5 copy-start
Sparse Core Ops, SparseCore 0:
  141.6 79.0 all-reduce.2
  386.8 35.9 reduce-scatter.1
where the time goes:
time: 431 us; the launch traced here: 430 us
  waiting for transfers between devices  258 us (60%)
  local copies, waits for them, and re-layouts  51.8 us (12%)
  other arithmetic  48.2 us (11%)
  matrix products  21.2 us (5%)
  blocking collectives  19.3 us (4%)
  starting transfers between devices  17.1 us (4%)
  between operations  13.6 us (3%)
    psum x1, waiting for transfers between devices, per_device(): smoothed = lax.psum(partial_sum, 'col')  79.2 us
    all_to_all x1, waiting for transfers between devices, per_device(): lax.all_to_all(prolong[asked_rows], 'space', split_axis=0, concat_axis=0,...  71.7 us
    all_to_all x1, waiting for transfers between devices, per_device(): lax.all_to_all(basis_tiles[asked_rows], 'space', split_axis=0, concat_axi...  71.3 us
    reduce_scatter x1, waiting for transfers between devices, per_device(): lax.psum_scatter(coarse_local, 'col', scatter_dimension=0, tiled=True)  36.2 us
    scatter-add x1, other arithmetic, per_device(): jax.ops.segment_sum(contribution.reshape(slot_total, coarse_size, coarse_...  31.5 us
    all_to_all x1, blocking collectives, per_device(): lax.all_to_all(requests, 'space', split_axis=0, concat_axis=0, tiled=True)  19.3 us
    reshape x1, local copies, waits for them, and re-layouts, per_device(): contribution.reshape(slot_total, coarse_size, coarse_size)  15.7 us
    gather x1, local copies, waits for them, and re-layouts, per_device(): prolong_table[tile_index]  11.1 us
  transfers between devices with their start and end apart: 4, of which 4 were waited for; matrix products, arithmetic and copies ran while one was open for 0% of the time, Pallas kernels for 0%

commit v1 on v0

--- a/solution.py
+++ b/solution.py
@@ -2,6 +2,7 @@
 import jax.numpy as jnp
 from jax import lax
 from jax.sharding import PartitionSpec as P
+from jax.lax import all_gather
 
 KC = 4
 CAP = 3
@@ -41,7 +42,11 @@
     usable = slot_number[None, :] < counts[:, None]
     masked = jnp.where(usable[:, :, None, None], blocks, jnp.zeros((), blocks.dtype))
     partial_sum = jnp.einsum("rkab,rkbc->rac", masked, fetched, preferred_element_type=jnp.float32)
-    smoothed = lax.psum(partial_sum, "col")
+
+    def lay_cycles(base_x, ax_name):
+        return jnp.sum(all_gather(base_x, ax_name), axis=0)
+
+    smoothed = lay_cycles(partial_sum, "col")
     prolong = (basis_tiles.astype(jnp.float32) - weights[:, :, None] * smoothed).astype(
         jnp.bfloat16
     )

time: 431 us -> 560 us (1.30)
  waiting for transfers between devices: 258 us -> 370 us
  other arithmetic: 48.2 us -> 65.4 us
    all_gather x0 -> x1, waiting for transfers between devices: none -> 193 us  [lay_cycles(): return jnp.sum(all_gather(base_x, ax_name), axis=0)]
    psum x1 -> x0, waiting for transfers between devices: 79.2 us -> none  [per_device(): smoothed = lax.psum(partial_sum, 'col')]
    reduce_sum x0 -> x1, other arithmetic: none -> 17.3 us  [lay_cycles(): return jnp.sum(all_gather(base_x, ax_name), axis=0)]
where the time goes in v1:
time: 560 us; the launch traced here: 559 us
  waiting for transfers between devices  370 us (66%)
  other arithmetic  65.4 us (12%)
  local copies, waits for them, and re-layouts  51.8 us (9%)
  matrix products  21.2 us (4%)
  blocking collectives  19.3 us (3%)
  starting transfers between devices  17.1 us (3%)
  between operations  13.6 us (2%)
    all_gather x1, waiting for transfers between devices, lay_cycles(): return jnp.sum(all_gather(base_x, ax_name), axis=0)  193 us
    all_to_all x1, waiting for transfers between devices, per_device(): lax.all_to_all(basis_tiles[asked_rows], 'space', split_axis=0, concat_axi...  71.3 us
    all_to_all x1, waiting for transfers between devices, per_device(): lax.all_to_all(prolong[asked_rows], 'space', split_axis=0, concat_axis=0,...  71.2 us
    reduce_scatter x1, waiting for transfers between devices, per_device(): lax.psum_scatter(coarse_local, 'col', scatter_dimension=0, tiled=True)  35 us
    scatter-add x1, other arithmetic, per_device(): jax.ops.segment_sum(contribution.reshape(slot_total, coarse_size, coarse_...  31.5 us
    all_to_all x1, blocking collectives, per_device(): lax.all_to_all(requests, 'space', split_axis=0, concat_axis=0, tiled=True)  19.3 us
    reduce_sum x1, other arithmetic, lay_cycles(): return jnp.sum(all_gather(base_x, ax_name), axis=0)  17.3 us
    reshape x1, local copies, waits for them, and re-layouts, per_device(): contribution.reshape(slot_total, coarse_size, coarse_size)  15.7 us
  transfers between devices with their start and end apart: 4, of which 4 were waited for; matrix products, arithmetic and copies ran while one was open for 0% of the time, Pallas kernels for 0%

profile of v1, /device:TPU:6, one launch (start us, length us, event | category | flops | bytes accessed | tf_op | source)
XLA Modules:
  0.0 558.7 jit_solution(11857731498358065532)
XLA Ops:
  6.5 0.8 copy.26
  7.3 0.7 broadcast_multiply_fusion
  8.0 0.8 copy.29
  8.8 0.2 reshape.182
  8.9 0.2 reshape.224
  9.1 0.2 eq.22
  9.2 0.7 broadcast_compare_fusion.1
  10.0 0.6 reduce-window.6
  10.6 0.2 slice_reduce_fusion
  10.8 0.1 bitcast_bitcast_fusion
  10.9 0.1 copy.24
  11.0 0.2 ne.29
  11.2 0.1 copy.25
  11.3 0.2 mul.47
  11.5 1.3 scatter_custom_fusion
  12.8 0.1 all_to_all.14
  12.9 19.3 %all_to_all.22 = s32[32,1,3]{2,1,0:T(1,128)S(1)} all-to-all(s32[32,1,3]{2,1,0:T(1,128)S(1)} %bitcast.46), channel_id=1, replica_groups=mesh['space'=32,'col'=8] {'space'}, dimensions={0} | all-to-all | bytes 768 | tf_op jit(solution)/shard_map/all_to_all | solution.py:32
  32.3 0.1 copy.31
  32.4 0.1 copy.32
  32.4 0.1 reshape.190
  32.6 0.0 copy-start.4
  32.6 0.0 copy-start.1
  32.6 4.6 gather_fusion
  37.2 6.6 %all-to-all-start.1 = ((bf16[32,3,128,128]{3,2,1,0:T(8,128)(2,1)}), bf16[32,3,128,128]{3,2,1,0:T(8,128)(2,1)}, u32[]{:S(2)}, u32[]{:S(2)}) async-start(bf16[32,3,128,128]{3,2,1,0:T(8,128)(2,1)} %bitcast.43), calls=%async_computation.1 | async-start | bytes 6291456 | tf_op jit(solution)/shard_map/all_to_all | solution.py:34
  43.9 0.0 all-gather.3.cloned.1.call-start
  43.9 0.0 copy-done.4
  44.0 0.1 broadcast_compare_fusion
  44.0 71.3 %all-to-all-done.1 = bf16[32,3,128,128]{3,2,1,0:T(8,128)(2,1)} async-done(((bf16[32,3,128,128]{3,2,1,0:T(8,128)(2,1)}), bf16[32,3,128,128]{3,2,1,0:T(8,128)(2,1)}, u32[]{:S(2)}, u32[]{:S(2)}) %all-to-all-start.1) | async-done | bytes 3145760 | tf_op jit(solution)/shard_map/all_to_all | solution.py:34
  115.3 0.0 copy-done.1
  115.3 4.9 pad_maximum_fusion
  120.2 11.1 %gather_fusion.1 = bf16[240,128,128]{2,1,0:T(8,128)(2,1)} fusion(bf16[176,128,128]{2,1,0:T(8,128)(2,1)} %pad_maximum_fusion, s32[1024]{0:T(1024)S(1)} %pad_clamp_fusion), kind=kCustom, calls=%fused_computation.1 | custom fusion | bytes 15729600 | tf_op jit(solution)/shard_map/gather | solution.py:40
  131.4 10.1 %fusion.8 = f32[80,128,128]{2,1,0:T(8,128)} fusion(bf16[80,3,128,128]{3,2,1,0:T(8,128)(2,1)} %bitcast.45, bf16[80,3,128,128]{3,2,1,0:T(8,128)(2,1)} %param.8, pred[80,3]{1,0:T(8,128)(4,1)S(1)} %broadcast_compare_fusion), kind=kOutput, calls=%fused_computation.17 | convolution fusion | flops 1010565120 | bytes 20971760 | tf_op jit(solution)/shard_map/rkab,rkbc->rac/dot_general | solution.py:44
  141.5 0.0 all-gather.3.cloned.1.call-update
  141.5 192.7 %all-gather.3.cloned.1.call-done = f32[640,128,128]{2,1,0:T(8,128)} async-done(((f32[80,128,128]{2,1,0:T(8,128)}), f32[640,128,128]{2,1,0:T(8,128)}) %all-gather.3.cloned.1.call-update) | async-done | bytes 41943056 | tf_op jit(solution)/shard_map/all_gather | solution.py:47
  334.2 0.0 copy-start.2
  334.2 17.3 %reduce_sum.22 = f32[80,128,128]{2,1,0:T(8,128)} reduce(f32[8,80,128,128]{3,2,1,0:T(8,128)} %bitcast.41, f32[]{:T(128)} %constant.12.clone.1), dimensions={0}, to_apply=%region_4.5 | reduce | flops 9175040 | bytes 47185924 | tf_op jit(solution)/shard_map/reduce_sum | solution.py:47
  351.4 0.0 copy-done.2
  351.4 4.6 subtract_convert_fusion
  356.0 0.0 copy-start.5
  356.1 0.0 copy-start.3
  356.1 2.7 gather_fusion.2
  358.8 10.2 %all-to-all-start.2 = ((bf16[32,3,128,128]{3,2,1,0:T(8,128)(2,1)}), bf16[32,3,128,128]{3,2,1,0:T(8,128)(2,1)}, u32[]{:S(2)}, u32[]{:S(2)}) async-start(bf16[32,3,128,128]{3,2,1,0:T(8,128)(2,1)} %bitcast.44), calls=%async_computation.2 | async-start | bytes 6291456 | tf_op jit(solution)/shard_map/all_to_all | solution.py:53
  369.0 0.2 reduce-scatter.2.cloned.1.call-start
  369.2 0.0 copy-done.5
  369.3 0.0 copy-done.3
  369.3 0.1 copy.23
  369.4 0.2 reshape.230
  369.5 71.2 %all-to-all-done.2 = bf16[32,3,128,128]{3,2,1,0:T(8,128)(2,1)} async-done(((bf16[32,3,128,128]{3,2,1,0:T(8,128)(2,1)}), bf16[32,3,128,128]{3,2,1,0:T(8,128)(2,1)}, u32[]{:S(2)}, u32[]{:S(2)}) %all-to-all-start.2) | async-done | bytes 3145760 | tf_op jit(solution)/shard_map/all_to_all | solution.py:53
  440.7 4.9 pad_maximum_fusion.1
  445.6 11.1 %gather_fusion.3 = bf16[240,128,128]{2,1,0:T(8,128)(2,1)} fusion(bf16[176,128,128]{2,1,0:T(8,128)(2,1)} %pad_maximum_fusion.1, s32[1024]{0:T(1024)S(1)} %pad_clamp_fusion), kind=kCustom, calls=%fused_computation.3 | custom fusion | bytes 15729600 | tf_op jit(solution)/shard_map/gather | solution.py:59
  456.7 11.1 %fusion = f32[80,3,128,128]{3,2,1,0:T(8,128)} fusion(bf16[80,3,128,128]{3,2,1,0:T(8,128)(2,1)} %bitcast.42, bf16[80,3,128,128]{3,2,1,0:T(8,128)(2,1)} %param.8, pred[80,3]{1,0:T(8,128)(4,1)S(1)} %broadcast_compare_fusion, bf16[80,128,128]{2,1,0:T(8,128)(2,1)S(1)} %subtract_convert_fusion), kind=kOutput, calls=%fused_computation.6 | convolution fusion | flops 2021130240 | bytes 34078960 | tf_op jit(solution)/shard_map/rad,rkae->rkde/dot_general | solution.py:65
  467.8 15.7 %copy.35 = f32[240,128,128]{2,1,0:T(8,128)} copy(f32[240,128,128]{1,2,0:T(8,128)} %bitcast.40) | data formatting | bytes 31457280 | tf_op jit(solution)/shard_map/reshape | solution.py:70
  483.5 0.3 broadcast_in_dim.20
  483.8 31.5 %scatter_fusion = f32[40,128,128]{2,1,0:T(8,128)S(1)} fusion(f32[40,128,128]{2,1,0:T(8,128)S(1)} %broadcast_in_dim.20, s32[240]{0:T(256)S(1)} %reshape.230, f32[240,128,128]{2,1,0:T(8,128)} %copy.35), kind=kCustom, calls=%fused_computation.5 | custom fusion | flops 3932160 | bytes 47186880 | tf_op jit(solution)/shard_map/scatter-add | solution.py:69
  515.3 0.0 copy-start
  515.3 1.5 copy-done
  516.8 0.0 reduce-scatter.2.cloned.1.call-update
  516.9 35.0 %reduce-scatter.2.cloned.1.call-done = f32[5,128,128]{2,1,0:T(8,128)} async-done(((f32[40,128,128]{2,1,0:T(8,128)}), f32[5,128,128]{2,1,0:T(8,128)}) %reduce-scatter.2.cloned.1.call-update) | async-done | bytes 327696 | tf_op jit(solution)/shard_map/reduce_scatter | solution.py:72
  (13 shorter events, 0.2 us)
Async XLA Ops:
  32.6 11.4 %copy-start.4 = (s32[80]{0:T(128)S(1)}, s32[80]{0:T(128)}, u32[]{:S(2)}) copy-start(s32[80]{0:T(128)} %param.13) | copy-start | bytes 964
  32.6 82.7 %copy-start.1 = (bf16[80,128,128]{2,1,0:T(8,128)(2,1)S(1)}, bf16[80,128,128]{2,1,0:T(8,128)(2,1)}, u32[]{:S(2)}) copy-start(bf16[80,128,128]{2,1,0:T(8,128)(2,1)} %param.9) | copy-start | bytes 7864324
  37.2 78.1 %all-to-all-start.1 = ((bf16[32,3,128,128]{3,2,1,0:T(8,128)(2,1)}), bf16[32,3,128,128]{3,2,1,0:T(8,128)(2,1)}, u32[]{:S(2)}, u32[]{:S(2)}) async-start(bf16[32,3,128,128]{3,2,1,0:T(8,128)(2,1)} %bitcast.43), calls=%async_computation.1 | async-start | bytes 6291456 | tf_op jit(solution)/shard_map/all_to_all | solution.py:34
  43.9 290.3 %all-gather.3.cloned.1.call-start = ((), (), s32[]{:S(2)}) async-start(), calls=%async_computation.5 | async-start | bytes 47185920 | tf_op jit(solution)/shard_map/all_gather | solution.py:47
  334.2 17.3 %copy-start.2 = (f32[80,128]{1,0:T(8,128)S(1)}, f32[80,128]{1,0:T(8,128)}, u32[]{:S(2)}) copy-start(f32[80,128]{1,0:T(8,128)} %param.10) | copy-start | bytes 122884
  356.0 13.2 %copy-start.5 = (s32[80]{0:T(128)S(1)}, s32[80]{0:T(128)}, u32[]{:S(2)}) copy-start(s32[80]{0:T(128)} %param.14) | copy-start | bytes 964
  356.1 13.2 %copy-start.3 = (s32[80,3]{0,1:T(4,128)S(1)}, s32[80,3]{0,1:T(4,128)}, u32[]{:S(2)}) copy-start(s32[80,3]{0,1:T(4,128)} %param.15) | copy-start | bytes 2884
  358.8 82.0 %all-to-all-start.2 = ((bf16[32,3,128,128]{3,2,1,0:T(8,128)(2,1)}), bf16[32,3,128,128]{3,2,1,0:T(8,128)(2,1)}, u32[]{:S(2)}, u32[]{:S(2)}) async-start(bf16[32,3,128,128]{3,2,1,0:T(8,128)(2,1)} %bitcast.44), calls=%async_computation.2 | async-start | bytes 6291456 | tf_op jit(solution)/shard_map/all_to_all | solution.py:53
  369.0 182.9 %reduce-scatter.2.cloned.1.call-start = ((), (), s32[]{:S(2)}) async-start(), calls=%async_computation.4 | async-start | bytes 2949120 | tf_op jit(solution)/shard_map/reduce_scatter | solution.py:72
  515.3 1.5 copy-start
Sparse Core Ops, SparseCore 0:
  141.6 192.5 all-gather.2
  517.0 34.8 reduce-scatter.1
